TPU v7x, 128 devices: a whole 4x4x4 slice. The times are simulated.
128 devices in a mesh: req: 16 (over y, z), mlp: 8 (over x, core).
Axes of the slice: x: 4, y: 4, z: 4, core: 2. Of those that a mesh axis runs over, the one named last changes fastest.
Arguments:
- blocks: bfloat16 [2048, 4096], P('req'), may hold values from -6 to 6
- token_embed: bfloat16 [2048, 4096], P('req'), may hold values from -6 to 6
- accepted: int32 [2048], P('req'), may hold values 0 or 1
- prompt_len: int32 [16], P('req'), may hold values from 2 to 512, as said below
- cache_len: int32 [16, 8], P('req'), may hold values from 1 to 1024, as said below
- prompt_kv: bfloat16 [16, 512, 2048], P('req', None, 'mlp'), may hold values from -364 to 364
- cache_kv: bfloat16 [16, 8, 1024, 2048], P('req', None, None, 'mlp'), may hold values from -6 to 6
- attn_gain: float32 [4096], replicated, may hold values from 0.25 to 1.75
- w_q: bfloat16 [4096, 4096], P(None, 'mlp'), may hold values from -0.09375 to 0.09375
- w_kv: bfloat16 [4096, 2048], P(None, 'mlp'), may hold values from -0.09375 to 0.09375
- w_o: bfloat16 [4096, 4096], P('mlp'), may hold values from -0.09375 to 0.09375
- mlp_gain: float32 [4096], replicated, may hold values from 0.25 to 1.75
- w_gate: bfloat16 [4096, 7168], P('req', 'mlp'), may hold values from -0.09375 to 0.09375
- w_up: bfloat16 [4096, 7168], P('req', 'mlp'), may hold values from -0.09375 to 0.09375
- w_down: bfloat16 [7168, 4096], P('mlp'), may hold values from -0.0625 to 0.0625
Outputs:
- denoised: bfloat16 [2048, 4096], P('req')
Inputs may be any that keep to these rules, and one draw needn't show every extreme that they name: `prompt_len`: shared by the 8 requests of a group; some group has a prompt of exactly 512. `cache_len`: every group has a request with exactly 1024 cached tokens.
All inputs are finite; a program needn't handle non-finite values. No bound on the sum of `accepted` on one device may be relied on, other than what follows from the above.
Results may differ from a plain program's by a relative error of at most 0.022.
Values may be sent and summed in bfloat16 or wider, within the bound.
A program may use at most 128 MiB of HBM per device.

v0:
```python
import math
import jax
import jax.numpy as jnp
from jax import lax
from jax.sharding import PartitionSpec as P

HEAD_DIM = 128
REQS = 8
BLOCK = 16
EPSILON = 1e-05
THETA = 500000.0


def rms_scale(stream, gain):
    widened = stream.astype(jnp.float32)
    mean_square = jnp.mean(widened * widened, axis=-1, keepdims=True)
    return (widened * lax.rsqrt(mean_square + EPSILON) * gain).astype(jnp.bfloat16)


def rope(values, positions):
    head_size = values.shape[-1]
    half_size = head_size // 2
    frequency = THETA ** (-2.0 * jnp.arange(half_size, dtype=jnp.float32) / head_size)
    angles = positions.astype(jnp.float32)[:, None] * frequency[None, :]
    cosine = jnp.cos(angles)[:, None, :]
    sine = jnp.sin(angles)[:, None, :]
    first = values[..., :half_size]
    second = values[..., half_size:]
    return jnp.concatenate(
        [first * cosine - second * sine, second * cosine + first * sine], axis=-1
    )


def attend_one(
    queries, block_keys, block_values, prompt_part, cached_part, prompt_size, cache_size
):
    block_len, head_count, head_size = queries.shape
    kv_heads = block_keys.shape[1]
    group_size = head_count // kv_heads
    grouped = queries.reshape(block_len, kv_heads, group_size, head_size)
    scale = 1.0 / math.sqrt(head_size)

    def scores(keys):
        return (
            jnp.einsum("tkgd,lkd->kgtl", grouped, keys, preferred_element_type=jnp.float32) * scale
        )

    prompt_score = scores(prompt_part[:, :, 0])
    cache_score = scores(cached_part[:, :, 0])
    block_score = scores(block_keys)
    prompt_ok = jnp.arange(prompt_part.shape[0], dtype=jnp.int32) < prompt_size
    cache_ok = jnp.arange(cached_part.shape[0], dtype=jnp.int32) < cache_size
    prompt_score = jnp.where(prompt_ok, prompt_score, -1e30)
    cache_score = jnp.where(cache_ok, cache_score, -1e30)
    largest = jnp.maximum(
        jnp.maximum(
            jnp.max(prompt_score, -1, keepdims=True), jnp.max(cache_score, -1, keepdims=True)
        ),
        jnp.max(block_score, -1, keepdims=True),
    )
    prompt_exp = jnp.exp(prompt_score - largest)
    cache_exp = jnp.exp(cache_score - largest)
    block_exp = jnp.exp(block_score - largest)
    total = (
        jnp.sum(prompt_exp, -1, keepdims=True)
        + jnp.sum(cache_exp, -1, keepdims=True)
        + jnp.sum(block_exp, -1, keepdims=True)
    )
    prompt_w = (prompt_exp / total).astype(jnp.bfloat16)
    cache_w = (cache_exp / total).astype(jnp.bfloat16)
    block_w = (block_exp / total).astype(jnp.bfloat16)
    result = jnp.einsum(
        "kgtl,lkd->tkgd", prompt_w, prompt_part[:, :, 1], preferred_element_type=jnp.float32
    )
    result = result + jnp.einsum(
        "kgtl,lkd->tkgd", cache_w, cached_part[:, :, 1], preferred_element_type=jnp.float32
    )
    result = result + jnp.einsum(
        "kgtl,lkd->tkgd", block_w, block_values, preferred_element_type=jnp.float32
    )
    return result.reshape(block_len, head_count * head_size).astype(jnp.bfloat16)


def swiglu(gate, up_part):
    return (jax.nn.silu(gate) * up_part).astype(jnp.bfloat16)


def body(
    blocks,
    token_embed,
    accepted,
    prompt_len,
    cache_len,
    prompt_kv,
    cache_kv,
    attn_gain,
    w_q,
    w_kv,
    w_o,
    mlp_gain,
    w_gate,
    w_up,
    w_down,
):
    row_count = blocks.shape[0]
    prompt_size = prompt_len[0]
    cache_sizes = cache_len[0]
    positions = (
        prompt_size + cache_sizes[:, None] + jnp.arange(BLOCK, dtype=jnp.int32)[None, :]
    ).reshape(-1)
    local_kv = w_kv.shape[1] // (2 * HEAD_DIM)
    local_heads = w_q.shape[1] // HEAD_DIM
    prompt_part = prompt_kv[0].reshape(-1, local_kv, 2, HEAD_DIM)
    cached = cache_kv[0].reshape(REQS, -1, local_kv, 2, HEAD_DIM)

    def one_pass(stream):
        normed = rms_scale(stream, attn_gain)
        queries = rope(
            jnp.dot(normed, w_q, preferred_element_type=jnp.float32).reshape(
                row_count, local_heads, HEAD_DIM
            ),
            positions,
        ).astype(jnp.bfloat16)
        key_value = jnp.dot(normed, w_kv, preferred_element_type=jnp.float32).reshape(
            row_count, local_kv, 2, HEAD_DIM
        )
        keys = rope(key_value[:, :, 0], positions).astype(jnp.bfloat16)
        values = key_value[:, :, 1].astype(jnp.bfloat16)

        def attend_request(items):
            query_part, key_part, value_part, cache_part, cache_size = items
            return attend_one(
                query_part, key_part, value_part, prompt_part, cache_part, prompt_size, cache_size
            )

        attended = lax.map(
            attend_request,
            (
                queries.reshape(REQS, BLOCK, local_heads, HEAD_DIM),
                keys.reshape(REQS, BLOCK, local_kv, HEAD_DIM),
                values.reshape(REQS, BLOCK, local_kv, HEAD_DIM),
                cached,
                cache_sizes,
            ),
        )
        attended = attended.reshape(row_count, local_heads * HEAD_DIM)
        mixed = lax.psum(jnp.dot(attended, w_o, preferred_element_type=jnp.float32), "mlp")
        after_attn = (stream.astype(jnp.float32) + mixed).astype(jnp.bfloat16)
        normed2 = rms_scale(after_attn, mlp_gain)
        pass_gate, pass_up = (
            lax.all_gather(w_gate, "req", axis=0, tiled=True),
            lax.all_gather(w_up, "req", axis=0, tiled=True),
        )
        gate = jnp.dot(normed2, pass_gate, preferred_element_type=jnp.float32)
        up_part = jnp.dot(normed2, pass_up, preferred_element_type=jnp.float32)
        hidden = swiglu(gate, up_part)
        down = lax.psum(jnp.dot(hidden, w_down, preferred_element_type=jnp.float32), "mlp")
        return (after_attn.astype(jnp.float32) + down).astype(jnp.bfloat16)

    first = one_pass(blocks)
    second_input = jnp.where(accepted[:, None] == 1, token_embed, first)
    return one_pass(second_input)


def solution(mesh):
    return jax.shard_map(
        body,
        mesh=mesh,
        in_specs=(
            P("req", None),
            P("req", None),
            P("req"),
            P("req"),
            P("req", None),
            P("req", None, "mlp"),
            P("req", None, None, "mlp"),
            P(),
            P(None, "mlp"),
            P(None, "mlp"),
            P("mlp", None),
            P(),
            P("req", "mlp"),
            P("req", "mlp"),
            P("mlp", None),
        ),
        out_specs=P("req", None),
        check_vma=False,
    )
```

profile of v0, /device:TPU:0, one launch (start us, length us, event | category | flops | bytes accessed | tf_op | source)
XLA Modules:
  0.0 504.8 jit_solution(11946350769607813790)
XLA Ops:
  7.4 1.7 fusion.76
  9.3 1.8 fusion.119
  12.8 2.9 fusion.121
  17.3 1.4 copy.63
  18.8 6.4 %copy.26 = bf16[1,8,1024,256]{2,3,1,0:T(8,128)(2,1)} copy(bf16[1,8,1024,256]{3,2,1,0:T(8,128)(2,1)} %param.25) | data formatting | bytes 8388608 | tf_op args[6]
  25.2 6.5 %copy.30 = bf16[8,1024,1,2,128]{4,1,3,2,0:T(8,128)(2,1)} copy(bf16[8,1024,1,2,128]{1,4,3,0,2:T(8,128)(2,1)} %bitcast.294) | data formatting | bytes 8388608 | tf_op jit(solution)/shard_map/while | solution.py:136
  33.1 45.7 %while.20 = (s32[]{:T(128)}, bf16[8,16,512]{2,1,0:T(8,128)(2,1)S(1)}, s32[]{:T(128)}, bf16[8,16,4,128]{3,1,0,2:T(8,128)(2,1)S(1)}, bf16[512,1,2,128]{3,0,2,1:T(8...) while((s32[]{:T(128)}, ...), condition=%wide.region_8.9_spmd, body=%wide.region_1.8_spmd.sunk | while | flops 51675520 | bytes 3347849 | solution.py:136
  33.1 1.1 dynamic-slice_bitcast_fusion.4
  38.8 1.1 dynamic-slice_bitcast_fusion.4
  44.5 1.1 dynamic-slice_bitcast_fusion.4
  50.2 1.1 dynamic-slice_bitcast_fusion.4
  56.0 1.1 dynamic-slice_bitcast_fusion.4
  61.7 1.1 dynamic-slice_bitcast_fusion.4
  78.8 4.2 fusion.154
  84.3 68.4 %all-reduce.5.cloned.1.call-done = f32[128,4096]{1,0:T(8,128)} async-done(((f32[128,4096]{1,0:T(8,128)}), f32[128,4096]{1,0:T(8,128)}) %all-reduce.5.cloned.1.call-update) | async-done | bytes 2097168 | tf_op jit(solution)/shard_map/psum | solution.py:147
  152.7 2.3 fusion.80
  155.5 5.2 %fusion.117 = f32[128,896]{1,0:T(8,128)} fusion(bf16[4096,896]{1,0:T(8,128)(2,1)} %all-gather.3.cloned.1.call-done, bf16[128,4096]{1,0:T(8,128)(2,1)S(1)} %get-tuple-element.160, f32[4096]{0:T(1024)S(1)} %copy-done.6, f32[128]{0:T(128)} %add_rsqrt_fusion.2), kind=kOutput, calls=%fused_computation.162 | convolution fusion | flops 941621248 | bytes 8864256 | tf_op jit(solution)/shard_map/dot_general | solution.py:154
  160.7 61.8 %all-gather.5.cloned.1.call-done = bf16[4096,896]{1,0:T(8,128)(2,1)} async-done(((bf16[256,896]{1,0:T(8,128)(2,1)}), bf16[4096,896]{1,0:T(8,128)(2,1)}) %all-gather.5.cloned.1.call-update) | async-done | bytes 7340048 | tf_op jit(solution)/shard_map/all_gather | solution.py:152
  222.5 9.0 %fusion.96 = f32[128,4096]{1,0:T(8,128)} fusion(bf16[896,4096]{1,0:T(8,128)(2,1)} %param.33, bf16[4096,896]{1,0:T(8,128)(2,1)} %all-gather.5.cloned.1.call-done, f32[128,896]{1,0:T(8,128)} %fusion.117, bf16[128,4096]{1,0:T(8,128)(2,1)S(1)} %get-tuple-element.160, f32[4096]{0:T(1024)S(1)} %copy-done.6, f32[128]{0:T(128)} %add_rsqrt_fusion.2), kind=kOutput, calls=%fused_computation.148 | convolution fusion | flops 1881833472 | bytes 18301440 | tf_op jit(solution)/shard_map/dot_general | solution.py:157
  231.8 1.2 broadcast_compare_fusion
  233.0 63.9 %all-reduce.7.cloned.1.call-done = f32[128,4096]{1,0:T(8,128)} async-done(((f32[128,4096]{1,0:T(8,128)}), f32[128,4096]{1,0:T(8,128)}) %all-reduce.7.cloned.1.call-update) | async-done | bytes 2097168 | tf_op jit(solution)/shard_map/psum | solution.py:157
  296.9 2.5 fusion.84
  301.1 3.3 fusion.113
  305.4 39.2 %while.21 = (s32[]{:T(128)}, bf16[8,16,512]{2,1,0:T(8,128)(2,1)S(1)}, s32[]{:T(128)}, bf16[8,16,4,128]{3,1,0,2:T(8,128)(2,1)S(1)}, bf16[512,1,2,128]{3,0,2,1:T(8...) while((s32[]{:T(128)}, ...), condition=%wide.region_20.21_spmd, body=%wide.region_13.20_spmd.sunk | while | flops 51675520 | bytes 3379597 | solution.py:136
  305.4 1.1 dynamic-slice_bitcast_fusion.5
  344.6 4.3 fusion.155
  348.9 65.2 %all-reduce.9.cloned.1.call-done = f32[128,4096]{1,0:T(8,128)} async-done(((f32[128,4096]{1,0:T(8,128)}), f32[128,4096]{1,0:T(8,128)}) %all-reduce.9.cloned.1.call-update) | async-done | bytes 2097168 | tf_op jit(solution)/shard_map/psum | solution.py:147
  414.2 2.0 fusion.88
  416.2 4.4 fusion.109
  420.6 9.0 %fusion.95 = f32[128,4096]{1,0:T(8,128)} fusion(bf16[896,4096]{1,0:T(8,128)(2,1)} %param.33, bf16[4096,896]{1,0:T(8,128)(2,1)} %all-gather.5.cloned.1.call-done, f32[128,896]{1,0:T(8,128)S(1)} %fusion.109, bf16[128,4096]{1,0:T(8,128)(2,1)S(1)} %get-tuple-element.156, f32[128]{0:T(128)S(1)} %add_rsqrt_fusion, f32[4096]{0:T(1024)S(1)} %copy-done.6), kind=kOutput, calls=%fused_computation.147 | convolution fusion | flops 1881833472 | bytes 18301440 | tf_op jit(solution)/shard_map/dot_general | solution.py:157
  429.6 65.3 %all-reduce.11.cloned.1.call-done = f32[128,4096]{1,0:T(8,128)} async-done(((f32[128,4096]{1,0:T(8,128)}), f32[128,4096]{1,0:T(8,128)}) %all-reduce.11.cloned.1.call-update) | async-done | bytes 2097168 | tf_op jit(solution)/shard_map/psum | solution.py:157
  494.9 2.8 fusion.91
  (360 shorter events, 84.9 us)
Async XLA Ops:
  7.4 1.9 copy-start
  7.4 145.3 %all-reduce.5.cloned.1.call-start = ((), (), s32[]{:S(2)}) async-start(), calls=%async_computation | async-start | bytes 4194304 | tf_op jit(solution)/shard_map/psum | solution.py:147
  7.4 9.0 %copy-start.9 = (f32[64]{0:T(128)}, f32[64]{0:T(128)S(1)}, u32[]{:S(2)}) copy-start(f32[64]{0:T(128)S(1)} %multiply_power_fusion) | copy-start | bytes 772
  9.3 3.3 copy-start.14
  9.3 3.5 copy-start.2
  9.3 3.5 copy-start.11
  12.8 3.6 copy-start.7
  25.2 6.5 %copy-start.5 = (bf16[1,512,256]{2,1,0:T(8,128)(2,1)S(1)}, bf16[1,512,256]{2,1,0:T(8,128)(2,1)}, u32[]{:S(2)}) copy-start(bf16[1,512,256]{2,1,0:T(8,128)(2,1)} %param.24) | copy-start | bytes 786436
  83.0 72.5 %all-gather.3.cloned.1.call-start = ((), (), s32[]{:S(2)}) async-start(), calls=%async_computation.1 | async-start | bytes 7798784 | tf_op jit(solution)/shard_map/all_gather | solution.py:151
  83.6 138.9 %all-gather.5.cloned.1.call-start = ((), (), s32[]{:S(2)}) async-start(), calls=%async_computation.2 | async-start | bytes 7798784 | tf_op jit(solution)/shard_map/all_gather | solution.py:152
  84.2 71.3 %copy-start.6 = (f32[4096]{0:T(1024)S(1)}, f32[4096]{0:T(1024)}, u32[]{:S(2)}) copy-start(f32[4096]{0:T(1024)} %param.30) | copy-start | bytes 49156
  84.2 212.6 %all-reduce.7.cloned.1.call-start = ((), (), s32[]{:S(2)}) async-start(), calls=%async_computation.3 | async-start | bytes 4194304 | tf_op jit(solution)/shard_map/psum | solution.py:157
  231.5 182.6 %all-reduce.9.cloned.1.call-start = ((), (), s32[]{:S(2)}) async-start(), calls=%async_computation.4 | async-start | bytes 4194304 | tf_op jit(solution)/shard_map/psum | solution.py:147
  296.9 3.5 copy-start.12
  299.4 1.0 copy-start.3
  300.3 0.7 copy-start.13
  301.1 3.3 copy-start.8
  301.1 3.3 copy-start.10
  304.4 1.0 copy-start.15
  348.8 65.3 %copy-start.4 = (bf16[128,4096]{1,0:T(8,128)(2,1)S(1)}, bf16[128,4096]{1,0:T(8,128)(2,1)}, u32[]{:S(2)}) copy-start(bf16[128,4096]{1,0:T(8,128)(2,1)} %copy-done.3) | copy-start | bytes 3145732
  348.9 146.0 %all-reduce.11.cloned.1.call-start = ((), (), s32[]{:S(2)}) async-start(), calls=%async_computation.5 | async-start | bytes 4194304 | tf_op jit(solution)/shard_map/psum | solution.py:157
  429.6 68.0 %copy-start.1 = (bf16[4096,256]{1,0:T(8,128)(2,1)S(1)}, bf16[4096,256]{1,0:T(8,128)(2,1)}, u32[]{:S(2)}) copy-start(bf16[4096,256]{1,0:T(8,128)(2,1)} %param.28) | copy-start | bytes 6291460
Sparse Core Ops, SparseCore 0:
  83.2 69.5 all-reduce.4
  231.7 65.1 all-reduce.6
  349.0 65.1 all-reduce.8
  429.7 65.1 all-reduce.10
Sparse Core Ops, SparseCore 1:
  85.7 68.7 all-gather.2
  156.6 65.9 all-gather.4
where the time goes:
time: 507 us; the launch traced here: 505 us
  waiting for transfers between devices  326 us (64%)
  matrix products  72.5 us (14%)
  local copies, waits for them, and re-layouts  45.8 us (9%)
  other arithmetic  43.5 us (9%)
  between operations  15.6 us (3%)
    psum x2, waiting for transfers between devices, one_pass(): lax.psum(jnp.dot(attended, w_o, preferred_element_type=jnp.float32), 'mlp')  134 us
    psum x2, waiting for transfers between devices, one_pass(): lax.psum(jnp.dot(hidden, w_down, preferred_element_type=jnp.float32), 'mlp')  129 us
    all_gather x1, waiting for transfers between devices, one_pass(): lax.all_gather(w_up, 'req', axis=0, tiled=True)  61.8 us
    dot_general x2, matrix products, one_pass(): jnp.dot(hidden, w_down, preferred_element_type=jnp.float32)  18 us
    squeeze x16, local copies, waits for them, and re-layouts, one_pass(): lax.map(attend_request, (queries.reshape(REQS, BLOCK, local_heads, HEAD_D...  17.3 us
    dot_general x48, matrix products, scores(): jnp.einsum('tkgd,lkd->kgtl', grouped, keys, preferred_element_type=jnp.fl...  11.7 us
    lt x16, other arithmetic, attend_one(): prompt_ok = jnp.arange(prompt_part.shape[0], dtype=jnp.int32) < prompt_size  10.5 us
    lt x16, other arithmetic, attend_one(): cache_ok = jnp.arange(cached_part.shape[0], dtype=jnp.int32) < cache_size  10.4 us
  transfers between devices with their start and end apart: 6, of which 5 were waited for; matrix products, arithmetic and copies ran while one was open for 2% of the time, Pallas kernels for 0%

commit v1 on v0

--- a/solution.py
+++ b/solution.py
@@ -9,6 +9,11 @@
 BLOCK = 16
 EPSILON = 1e-05
 THETA = 500000.0
+
+
+def all_by_exchange(array, mesh_axis, dim):
+    repeated = jnp.stack([array] * lax.axis_size(mesh_axis))
+    return jnp.concatenate(lax.all_to_all(repeated, mesh_axis, 0, 0), axis=dim)
 
 
 def rms_scale(stream, gain):
@@ -149,7 +154,7 @@
         normed2 = rms_scale(after_attn, mlp_gain)
         pass_gate, pass_up = (
             lax.all_gather(w_gate, "req", axis=0, tiled=True),
-            lax.all_gather(w_up, "req", axis=0, tiled=True),
+            all_by_exchange(w_up, "req", 0),
         )
         gate = jnp.dot(normed2, pass_gate, preferred_element_type=jnp.float32)
         up_part = jnp.dot(normed2, pass_up, preferred_element_type=jnp.float32)

time: 507 us -> 551 us (1.087)
  waiting for transfers between devices: 326 us -> 348 us
  local copies, waits for them, and re-layouts: 45.8 us -> 55.8 us
  starting transfers between devices: 0.39 us -> 8.51 us
    all_gather x1, waiting for transfers between devices: 0.01 us -> 92.3 us  [one_pass(): lax.all_gather(w_gate, 'req', axis=0, tiled=True)]
    all_gather x1 -> x0, waiting for transfers between devices: 61.8 us -> none  [one_pass(): lax.all_gather(w_up, 'req', axis=0, tiled=True)]
    psum x2, waiting for transfers between devices: 134 us -> 122 us  [one_pass(): lax.psum(jnp.dot(attended, w_o, preferred_element_type=jnp.float32), 'mlp')]
    all_to_all x0 -> x1, starting transfers between devices: none -> 8.16 us  [all_by_exchange(): return jnp.concatenate(lax.all_to_all(repeated, mesh_axis, 0, 0), axis=dim)]
    dot_general x16, matrix products: 8.76 us -> 14.3 us  [attend_one(): jnp.einsum('kgtl,lkd->tkgd', block_w, block_values, preferred_element_typ...]
where the time goes in v1:
time: 551 us; the launch traced here: 549 us
  waiting for transfers between devices  348 us (63%)
  matrix products  77.5 us (14%)
  local copies, waits for them, and re-layouts  55.8 us (10%)
  other arithmetic  42.7 us (8%)
  between operations  15.6 us (3%)
  starting transfers between devices  8.51 us (2%)
    psum x2, waiting for transfers between devices, one_pass(): lax.psum(jnp.dot(hidden, w_down, preferred_element_type=jnp.float32), 'mlp')  133 us
    psum x2, waiting for transfers between devices, one_pass(): lax.psum(jnp.dot(attended, w_o, preferred_element_type=jnp.float32), 'mlp')  122 us
    all_gather x1, waiting for transfers between devices, one_pass(): lax.all_gather(w_gate, 'req', axis=0, tiled=True)  92.3 us
    dot_general x2, matrix products, one_pass(): jnp.dot(hidden, w_down, preferred_element_type=jnp.float32)  18.3 us
    squeeze x16, local copies, waits for them, and re-layouts, one_pass(): lax.map(attend_request, (queries.reshape(REQS, BLOCK, local_heads, HEAD_D...  17.3 us
    dynamic_slice x16, local copies, waits for them, and re-layouts, one_pass(): lax.map(attend_request, (queries.reshape(REQS, BLOCK, local_heads, HEAD_D...  15.7 us
    dot_general x16, matrix products, attend_one(): jnp.einsum('kgtl,lkd->tkgd', block_w, block_values, preferred_element_typ...  14.3 us
    dot_general x48, matrix products, scores(): jnp.einsum('tkgd,lkd->kgtl', grouped, keys, preferred_element_type=jnp.fl...  11.7 us
  transfers between devices with their start and end apart: 6, of which 5 were waited for; matrix products, arithmetic and copies ran while one was open for 2% of the time, Pallas kernels for 0%

profile of v1, /device:TPU:0, one launch (start us, length us, event | category | flops | bytes accessed | tf_op | source)
XLA Modules:
  0.0 548.7 jit_solution(9528408026434702988)
XLA Ops:
  7.4 1.7 fusion.76
  9.3 1.8 fusion.119
  11.9 3.7 fusion.121
  18.0 6.5 %copy.26 = bf16[1,8,1024,256]{2,3,1,0:T(8,128)(2,1)} copy(bf16[1,8,1024,256]{3,2,1,0:T(8,128)(2,1)} %param.25) | data formatting | bytes 8388608 | tf_op args[6]
  24.4 6.5 %copy.30 = bf16[8,1024,1,2,128]{4,1,3,2,0:T(8,128)(2,1)} copy(bf16[8,1024,1,2,128]{1,4,3,0,2:T(8,128)(2,1)} %bitcast.295) | data formatting | bytes 8388608 | tf_op jit(solution)/shard_map/while | solution.py:141
  32.6 45.0 %while.20 = (s32[]{:T(128)}, bf16[8,16,512]{2,1,0:T(8,128)(2,1)S(1)}, s32[]{:T(128)}, bf16[8,16,4,128]{3,1,0,2:T(8,128)(2,1)S(1)}, bf16[512,1,2,128]{3,0,2,1:T(8...) while((s32[]{:T(128)}, ...), condition=%wide.region_8.9_spmd, body=%wide.region_1.8_spmd.sunk | while | flops 51675520 | bytes 3347349 | solution.py:141
  77.6 4.3 fusion.154
  82.9 4.0 stack.2
  86.9 8.2 %all-to-all-start = ((bf16[16,256,896]{2,1,0:T(8,128)(2,1)}), bf16[16,256,896]{2,1,0:T(8,128)(2,1)}, u32[]{:S(2)}, u32[]{:S(2)}) async-start(bf16[16,256,896]{2,1,0:T(8,128)(2,1)} %stack.2), calls=%async_computation | async-start | bytes 14680064 | tf_op jit(solution)/shard_map/all_to_all | solution.py:16
  95.1 56.7 %all-reduce.5.cloned.1.call-done = f32[128,4096]{1,0:T(8,128)} async-done(((f32[128,4096]{1,0:T(8,128)}), f32[128,4096]{1,0:T(8,128)}) %all-reduce.5.cloned.1.call-update) | async-done | bytes 2097168 | tf_op jit(solution)/shard_map/psum | solution.py:152
  151.8 2.3 fusion.80
  154.7 92.3 %all-gather.2.cloned.1.call-done = bf16[4096,896]{1,0:T(8,128)(2,1)} async-done(((bf16[256,896]{1,0:T(8,128)(2,1)}), bf16[4096,896]{1,0:T(8,128)(2,1)}) %all-gather.2.cloned.1.call-update) | async-done | bytes 7340048 | tf_op jit(solution)/shard_map/all_gather | solution.py:156
  247.0 5.2 fusion.117
  252.2 9.1 %fusion.96 = f32[128,4096]{1,0:T(8,128)} fusion(bf16[896,4096]{1,0:T(8,128)(2,1)} %param.33, bf16[4096,896]{1,0:T(8,128)(2,1)} %bitcast.70, f32[128,896]{1,0:T(8,128)} %fusion.117, bf16[128,4096]{1,0:T(8,128)(2,1)S(1)} %get-tuple-element.160, f32[4096]{0:T(1024)S(1)} %copy-done.7, f32[128]{0:T(128)} %add_rsqrt_fusion.2), kind=kOutput, calls=%fused_computation.148 | convolution fusion | flops 1881833472 | bytes 18301440 | tf_op jit(solution)/shard_map/dot_general | solution.py:162
  262.7 67.5 %all-reduce.7.cloned.1.call-done = f32[128,4096]{1,0:T(8,128)} async-done(((f32[128,4096]{1,0:T(8,128)}), f32[128,4096]{1,0:T(8,128)}) %all-reduce.7.cloned.1.call-update) | async-done | bytes 2097168 | tf_op jit(solution)/shard_map/psum | solution.py:162
  330.2 2.7 fusion.84
  336.5 50.9 %while.21 = (s32[]{:T(128)}, bf16[8,16,512]{2,1,0:T(8,128)(2,1)S(1)}, s32[]{:T(128)}, bf16[8,16,4,128]{3,1,0,2:T(8,128)(2,1)S(1)}, bf16[512,1,2,128]{3,0,2,1:T(8...) while((s32[]{:T(128)}, ...), condition=%wide.region_20.21_spmd, body=%wide.region_13.20_spmd.sunk | while | flops 51675520 | bytes 3347349 | solution.py:141
  337.6 1.3 dynamic_slice.119
  343.9 1.3 dynamic_slice.119
  350.3 1.3 dynamic_slice.119
  356.6 1.3 dynamic_slice.119
  363.0 1.3 dynamic_slice.119
  369.4 1.3 dynamic_slice.119
  375.7 1.3 dynamic_slice.119
  382.1 1.3 dynamic_slice.119
  387.4 4.3 fusion.155
  391.7 65.2 %all-reduce.9.cloned.1.call-done = f32[128,4096]{1,0:T(8,128)} async-done(((f32[128,4096]{1,0:T(8,128)}), f32[128,4096]{1,0:T(8,128)}) %all-reduce.9.cloned.1.call-update) | async-done | bytes 2097168 | tf_op jit(solution)/shard_map/psum | solution.py:152
  456.9 2.3 fusion.88
  459.2 5.2 fusion.109
  464.4 9.2 %fusion.95 = f32[128,4096]{1,0:T(8,128)} fusion(bf16[896,4096]{1,0:T(8,128)(2,1)} %param.33, bf16[4096,896]{1,0:T(8,128)(2,1)} %bitcast.70, f32[128,896]{1,0:T(8,128)} %fusion.109, bf16[128,4096]{1,0:T(8,128)(2,1)S(1)} %get-tuple-element.156, f32[128]{0:T(128)S(1)} %add_rsqrt_fusion, f32[4096]{0:T(1024)S(1)} %copy-done.7), kind=kOutput, calls=%fused_computation.147 | convolution fusion | flops 1881833472 | bytes 18301440 | tf_op jit(solution)/shard_map/dot_general | solution.py:162
  473.5 65.3 %all-reduce.11.cloned.1.call-done = f32[128,4096]{1,0:T(8,128)} async-done(((f32[128,4096]{1,0:T(8,128)}), f32[128,4096]{1,0:T(8,128)}) %all-reduce.11.cloned.1.call-update) | async-done | bytes 2097168 | tf_op jit(solution)/shard_map/psum | solution.py:162
  538.8 2.8 fusion.91
  (359 shorter events, 95.1 us)
Async XLA Ops:
  7.4 1.9 copy-start
  7.4 144.4 %all-reduce.5.cloned.1.call-start = ((), (), s32[]{:S(2)}) async-start(), calls=%async_computation.1 | async-start | bytes 4194304 | tf_op jit(solution)/shard_map/psum | solution.py:152
  7.4 23.9 %copy-start.10 = (f32[64]{0:T(128)}, f32[64]{0:T(128)S(1)}, u32[]{:S(2)}) copy-start(f32[64]{0:T(128)S(1)} %multiply_power_fusion) | copy-start | bytes 772
  9.3 2.6 copy-start.1
  11.2 4.4 copy-start.3
  11.9 5.6 %copy-start.14 = (s32[1,8]{1,0:T(1,128)S(1)}, s32[1,8]{1,0:T(1,128)}, u32[]{:S(2)}) copy-start(s32[1,8]{1,0:T(1,128)} %param.23) | copy-start | bytes 100
  11.9 5.8 %copy-start.5 = (bf16[1,512,256]{2,1,0:T(8,128)(2,1)S(1)}, bf16[1,512,256]{2,1,0:T(8,128)(2,1)}, u32[]{:S(2)}) copy-start(bf16[1,512,256]{2,1,0:T(8,128)(2,1)} %param.24) | copy-start | bytes 786436
  17.7 13.6 %copy-start.8 = (f32[128]{0:T(128)}, f32[128]{0:T(128)S(1)}, u32[]{:S(2)}) copy-start(f32[128]{0:T(128)S(1)} %convert_element_type.168) | copy-start | bytes 1540
  24.4 6.9 %slice-start = ((f32[128,1,2,128]{3,2,0,1:T(2,128)}), f32[128,1,1,128]{3,2,0,1:T(1,128)S(1)}, s32[]{:S(2)}) async-start(f32[128,1,2,128]{3,2,0,1:T(2,128)} %copy-done.3), calls=%async_computation.6 | async-start | bytes 131072 | tf_op jit(solution)/shard_map/slice | solution.py:132
  24.4 7.2 %copy-start.6 = (bf16[128,1,1,128]{3,2,0,1:T(2,128)(2,1)S(1)}, bf16[128,1,1,128]{3,2,0,1:T(2,128)(2,1)}, u32[]{:S(2)}) copy-start(bf16[128,1,1,128]{3,2,0,1:T(2,128)(2,1)} %slice.83) | copy-start | bytes 98308
  81.9 1.0 copy-start.4
  81.9 165.0 %all-gather.2.cloned.1.call-start = ((), (), s32[]{:S(2)}) async-start(), calls=%async_computation.2 | async-start | bytes 7798784 | tf_op jit(solution)/shard_map/all_gather | solution.py:156
  86.9 165.3 %all-to-all-start = ((bf16[16,256,896]{2,1,0:T(8,128)(2,1)}), bf16[16,256,896]{2,1,0:T(8,128)(2,1)}, u32[]{:S(2)}, u32[]{:S(2)}) async-start(bf16[16,256,896]{2,1,0:T(8,128)(2,1)} %stack.2), calls=%async_computation | async-start | bytes 14680064 | tf_op jit(solution)/shard_map/all_to_all | solution.py:16
  95.1 151.9 %copy-start.7 = (f32[4096]{0:T(1024)S(1)}, f32[4096]{0:T(1024)}, u32[]{:S(2)}) copy-start(f32[4096]{0:T(1024)} %param.30) | copy-start | bytes 49156
  95.1 235.1 %all-reduce.7.cloned.1.call-start = ((), (), s32[]{:S(2)}) async-start(), calls=%async_computation.3 | async-start | bytes 4194304 | tf_op jit(solution)/shard_map/psum | solution.py:162
  261.3 195.6 %all-reduce.9.cloned.1.call-start = ((), (), s32[]{:S(2)}) async-start(), calls=%async_computation.4 | async-start | bytes 4194304 | tf_op jit(solution)/shard_map/psum | solution.py:152
  330.2 3.1 copy-start.12
  330.2 3.1 copy-start.13
  332.8 1.3 copy-start.2
  334.2 1.1 copy-start.9
  334.2 1.1 copy-start.11
  391.6 147.2 %all-reduce.11.cloned.1.call-start = ((), (), s32[]{:S(2)}) async-start(), calls=%async_computation.5 | async-start | bytes 4194304 | tf_op jit(solution)/shard_map/psum | solution.py:162
Sparse Core Ops, SparseCore 0:
  82.1 69.6 all-reduce.4
  261.4 68.7 all-reduce.6
  391.8 65.1 all-reduce.8
  473.7 65.1 all-reduce.10
Sparse Core Ops, SparseCore 1:
  84.6 162.3 all-gather.1
